TPU v7x, 32 devices: a whole 2x2x4 slice. The times are simulated.
32 devices in a mesh: dp: 4 (over y, x), section: 2 (over core), tensor: 4 (over z).
Axes of the slice: x: 2, y: 2, z: 4, core: 2. Of those that a mesh axis runs over, the one named last changes fastest.
Arguments:
- stored: bfloat16 [2, 2, 256, 8192], P('section', None, 'dp', 'tensor'), may hold values from -6 to 6
- cotangent: bfloat16 [2, 32, 8192], P(None, None, 'tensor'), may hold values from -12 to 12
- positions: int32 [2, 32], replicated, may hold values from 128 to 255, as said below
- lengths: int32 [2], replicated, may hold values from 128 to 256, as said below
- norm_gain: float32 [2, 8192], P('section'), may hold values from 0.5 to 1.5
- w_query: bfloat16 [2, 8192, 8192], P('section', None, 'tensor')
- w_key: bfloat16 [2, 8192, 1024], P('section', None, 'tensor')
- w_value: bfloat16 [2, 8192, 1024], P('section', None, 'tensor'), may hold values from -0.0625 to 0.0625
- w_out: bfloat16 [2, 8192, 8192], P('section', 'tensor', 'dp'), may hold values from -0.0625 to 0.0625
Outputs:
- input_grads: float32 [2, 2, 256, 8192], P('section', None, 'dp', 'tensor')
Inputs may be any that keep to these rules, and one draw needn't show every extreme that they name: In each sequence the response positions are distinct, rise along the last dimension, lie in the last 128 positions, and the last one is 255. `lengths`: some sequence has length 256.
All inputs are finite; a program needn't handle non-finite values.
Results may differ from a plain program's by a relative error of at most 0.017.
Values may be sent and summed in bfloat16 or wider, within the bound.
A program may use at most 256 MiB of HBM per device.

v0:
```python
import math
import jax
import jax.numpy as jnp
from jax import lax
from jax.sharding import PartitionSpec as P

HD = 128
EPS = 1e-05
THETA = 500000.0


def passed_along(value, axis, steps):
    count = lax.axis_size(axis)
    leading, last = (max(0, -steps), min(count, count - steps))
    return lax.ppermute(value, axis, [(source, source + steps) for source in range(leading, last)])


def angle_tables(row_places):
    half_dim = HD // 2
    frequency = THETA ** (-(jnp.arange(half_dim, dtype=jnp.float32) * 2.0) / HD)
    angles = row_places[:, None] * frequency[None, :]
    cosine = jnp.concatenate([jnp.cos(angles), jnp.cos(angles)], -1)[:, None, :]
    sine_table = jnp.concatenate([jnp.sin(angles), jnp.sin(angles)], -1)[:, None, :]
    return (cosine, sine_table)


def turn_half(values):
    half_dim = values.shape[-1] // 2
    return jnp.concatenate([-values[..., half_dim:], values[..., :half_dim]], -1)


def rotate(values, cosine, sine_table):
    return values * cosine + turn_half(values) * sine_table


def unrotate(values, cosine, sine_table):
    return values * cosine - turn_half(values * sine_table)


def layer_grad(own_input, own_upstream, seq_lengths, gain, w_query, w_key, w_value, w_out):
    batch, rows, width_dev = own_input.shape
    kv_dev = w_key.shape[1] // HD
    q_dev = w_query.shape[1] // HD
    group = q_dev // kv_dev
    scale = 1.0 / math.sqrt(HD)
    x_whole, g_whole = (
        lax.all_gather(own_input, "tensor", axis=2, tiled=True),
        lax.all_gather(own_upstream, "tensor", axis=2, tiled=True),
    )
    width = x_whole.shape[2]
    x_full = x_whole.astype(jnp.float32)
    inv_rms = lax.rsqrt(jnp.mean(x_full * x_full, -1, keepdims=True) + EPS)
    normed = (x_full * inv_rms * gain).astype(jnp.bfloat16)
    first_row = lax.axis_index("dp") * rows
    query_ids = first_row + jnp.arange(rows, dtype=jnp.int32)
    cosine, sine_table = angle_tables(query_ids.astype(jnp.float32))
    queries = jnp.einsum(
        "bpd,dc->bpc", normed, w_query, preferred_element_type=jnp.float32
    ).reshape(batch, rows, q_dev, HD)
    keys = jnp.einsum("bpd,dc->bpc", normed, w_key, preferred_element_type=jnp.float32).reshape(
        batch, rows, kv_dev, HD
    )
    values = jnp.einsum("bpd,dc->bpc", normed, w_value, preferred_element_type=jnp.float32).reshape(
        batch, rows, kv_dev, HD
    )
    q_rot = rotate(queries, cosine, sine_table).astype(jnp.bfloat16)
    k_rot = rotate(keys, cosine, sine_table).astype(jnp.bfloat16)
    values_b = values.astype(jnp.bfloat16)
    grad_out = jnp.einsum("bpd,cd->bpc", g_whole, w_out, preferred_element_type=jnp.float32).astype(
        jnp.bfloat16
    )
    all_keys, all_values = (
        lax.all_gather(k_rot, "dp", axis=1, tiled=True),
        lax.all_gather(values_b, "dp", axis=1, tiled=True),
    )
    length = all_keys.shape[1]
    q_five = q_rot.reshape(batch, rows, kv_dev, group, HD)
    o_five = grad_out.reshape(batch, rows, kv_dev, group, HD)
    key_ids = jnp.arange(length, dtype=jnp.int32)
    causal = key_ids[None, None, :] <= query_ids[None, :, None]
    start_pos = length - seq_lengths
    inside = (key_ids[None, None, :] >= start_pos[:, None, None]) | (
        key_ids[None, None, :] == query_ids[None, :, None]
    )
    allowed = (causal & inside)[:, None, None, :, :]
    scores = (
        jnp.einsum("bpkgd,bjkd->bkgpj", q_five, all_keys, preferred_element_type=jnp.float32)
        * scale
    )
    masked = jnp.where(allowed, scores, -1e30)
    highest = jnp.max(masked, -1, keepdims=True)
    expo_terms = jnp.where(allowed, jnp.exp(masked - highest), 0.0)
    probs = expo_terms / jnp.sum(expo_terms, -1, keepdims=True)
    grad_probs = jnp.einsum(
        "bpkgd,bjkd->bkgpj", o_five, all_values, preferred_element_type=jnp.float32
    )
    row_dot = jnp.sum(probs * grad_probs, -1, keepdims=True)
    grad_scores = (probs * (grad_probs - row_dot) * scale).astype(jnp.bfloat16)
    probs_b = probs.astype(jnp.bfloat16)
    grad_qr = jnp.einsum(
        "bkgpj,bjkd->bpkgd", grad_scores, all_keys, preferred_element_type=jnp.float32
    )
    key_terms = jnp.einsum(
        "bkgpj,bpkgd->bjkd", grad_scores, q_five, preferred_element_type=jnp.float32
    )
    value_terms = jnp.einsum(
        "bkgpj,bpkgd->bjkd", probs_b, o_five, preferred_element_type=jnp.float32
    )
    grad_kr, grad_vr = (
        lax.psum_scatter(
            key_terms.astype(jnp.bfloat16), "dp", scatter_dimension=1, tiled=True
        ).astype(jnp.float32),
        lax.psum_scatter(
            value_terms.astype(jnp.bfloat16), "dp", scatter_dimension=1, tiled=True
        ).astype(jnp.float32),
    )
    grad_q = (
        unrotate(grad_qr.reshape(batch, rows, q_dev, HD), cosine, sine_table)
        .astype(jnp.bfloat16)
        .reshape(batch, rows, q_dev * HD)
    )
    grad_k = (
        unrotate(grad_kr, cosine, sine_table).astype(jnp.bfloat16).reshape(batch, rows, kv_dev * HD)
    )
    grad_v = grad_vr.astype(jnp.bfloat16).reshape(batch, rows, kv_dev * HD)
    partial_term = jnp.einsum("bpc,dc->bpd", grad_q, w_query, preferred_element_type=jnp.float32)
    partial_term = partial_term + jnp.einsum(
        "bpc,dc->bpd", grad_k, w_key, preferred_element_type=jnp.float32
    )
    partial_term = partial_term + jnp.einsum(
        "bpc,dc->bpd", grad_v, w_value, preferred_element_type=jnp.float32
    )
    summed = lax.psum(partial_term.astype(jnp.bfloat16), "tensor").astype(jnp.float32)
    stat = jnp.sum(x_full * gain * summed, -1, keepdims=True)
    whole_grad = (
        g_whole.astype(jnp.float32) + inv_rms * gain * summed - x_full * inv_rms**3 * stat / width
    )
    return lax.dynamic_slice_in_dim(whole_grad, lax.axis_index("tensor") * width_dev, width_dev, 2)


def on_device(stored, cotangent, positions, lengths, norm_gain, w_query, w_key, w_value, w_out):
    own_input = stored[0]
    gain = norm_gain[0]
    wq_layer = w_query[0]
    wk_layer = w_key[0]
    wv_layer = w_value[0]
    wo_layer = lax.all_gather(w_out[0], "dp", axis=1, tiled=True)
    seqs, rows, width_dev = own_input.shape
    section_id = lax.axis_index("section")
    row_ids = lax.axis_index("dp") * rows + jnp.arange(rows, dtype=jnp.int32)
    placed = (positions[:, None, :] == row_ids[None, :, None]).astype(jnp.bfloat16)
    from_loss = jnp.einsum(
        "spr,srd->spd", placed, cotangent, preferred_element_type=jnp.float32
    ).astype(jnp.bfloat16)

    def run_layer(input_part, upstream_part, length_part):
        return layer_grad(
            input_part, upstream_part, length_part, gain, wq_layer, wk_layer, wv_layer, wo_layer
        )

    first_in = jnp.where(section_id == 1, from_loss, jnp.zeros_like(from_loss))
    first_pass = run_layer(own_input, first_in, lengths)
    handed = passed_along(first_pass.astype(jnp.bfloat16), "section", -1)
    second_pass = run_layer(own_input, handed, lengths)
    result = jnp.where(section_id == 0, second_pass, first_pass)
    return result[None]


def solution(mesh):
    return jax.shard_map(
        on_device,
        mesh=mesh,
        in_specs=(
            P("section", None, "dp", "tensor"),
            P(None, None, "tensor"),
            P(),
            P(),
            P("section", None),
            P("section", None, "tensor"),
            P("section", None, "tensor"),
            P("section", None, "tensor"),
            P("section", "tensor", "dp"),
        ),
        out_specs=P("section", None, "dp", "tensor"),
        check_vma=False,
    )
```

profile of v0, /device:TPU:0, one launch (start us, length us, event | category | flops | bytes accessed | tf_op | source)
XLA Modules:
  0.0 914.5 jit_solution(1680415631563956756)
XLA Ops:
  6.5 0.7 all-gather.11.cloned.1.call-update
  7.5 2.0 fusion.50
  9.5 0.7 all-gather.13.cloned.1.call-update
  10.3 40.0 %copy.63 = bf16[2048,8192]{1,0:T(8,128)(2,1)} copy(bf16[2048,8192]{0,1:T(8,128)(2,1)} %bitcast.235) | data formatting | bytes 67108864 | tf_op jit(solution)/shard_map/bpd,dc->bpc/dot_general | solution.py:57
  50.3 6.4 copy.62
  56.7 6.4 copy.64
  63.1 0.6 dynamic-slice
  64.9 2.3 fusion.33
  67.4 3.9 fusion.117
  71.5 10.4 %all_gather.23 = bf16[2,256,2,128]{3,1,2,0:T(8,128)(2,1)S(1)} all-gather(bf16[2,64,2,128]{3,1,2,0:T(8,128)(2,1)S(1)} %fusion.113), channel_id=1, replica_groups=mesh['dp'=4,'section'=2,'tensor'=4] {'dp'}, dimensions={1}, use_global_device_ids=true | all-gather | bytes 327680 | tf_op jit(solution)/shard_map/all_gather | solution.py:73
  81.9 1.5 convolution_convert_fusion.1
  83.4 9.6 %all_gather.24 = bf16[2,256,2,128]{3,1,2,0:T(8,128)(2,1)S(1)} all-gather(bf16[2,64,2,128]{3,1,2,0:T(8,128)(2,1)S(1)} %convolution_convert_fusion.1), channel_id=1, replica_groups=mesh['dp'=4,'section'=2,'tensor'=4] {'dp'}, dimensions={1}, use_global_device_ids=true | all-gather | bytes 327680 | tf_op jit(solution)/shard_map/all_gather | solution.py:74
  93.1 15.8 %fusion.115 = f32[2,64,16,128]{3,1,2,0:T(8,128)S(1)} fusion(bf16[16,128,8192,1]{2,1,0,3:T(8,128)(2,1)} %bitcast.236, bf16[1,2,64,8192]{3,2,1,0:T(8,128)(2,1)S(1)} %copy-done.2, f32[8192]{0:T(1024)S(1)} %bitcast.253, f32[2,64]{1,0:T(2,128)S(1)} %get-tuple-element.23), kind=kOutput, calls=%fused_computation.131 | convolution fusion | flops 4299161600 | bytes 36733440 | tf_op jit(solution)/shard_map/bpd,dc->bpc/dot_general | solution.py:57
  108.9 0.4 slice_negate_fusion.2
  109.3 0.4 fusion.74
  109.7 2.3 fusion.146
  112.0 3.8 fusion.143
  115.8 285.4 %all-gather.13.cloned.1.call-done = bf16[1,2048,8192]{2,1,0:T(8,128)(2,1)} async-done(((bf16[1,2048,2048]{2,1,0:T(8,128)(2,1)}), bf16[1,2048,8192]{2,1,0:T(8,128)(2,1)}) %all-gather.13.cloned.1.call-update) | async-done | bytes 33554448 | tf_op jit(solution)/shard_map/all_gather | solution.py:147
  401.2 16.4 %fusion.44 = bf16[2,64,2048]{2,1,0:T(8,128)(2,1)S(1)} fusion(bf16[2,64,8192]{2,1,0:T(8,128)(2,1)} %all-gather.7.cloned.1.call-done, bf16[1,2048,8192]{2,1,0:T(8,128)(2,1)} %all-gather.13.cloned.1.call-done), kind=kOutput, calls=%fused_computation.36 | convolution fusion | flops 4295229440 | bytes 36175872 | tf_op jit(solution)/shard_map/bpd,cd->bpc/dot_general | solution.py:69
  417.7 0.8 copy-done.13
  418.5 1.7 fusion.96
  420.2 15.5 %fusion.77 = f32[2,2,128,8,64]{2,4,3,1,0:T(8,128)} fusion(f32[2,2,256,64,8]{2,3,4,1,0:T(8,128)} %fusion.96, bf16[2,256,2,128]{3,1,2,0:T(8,128)(2,1)S(1)} %all_gather.23, f32[2,2,8,64,256]{4,3,2,1,0:T(8,128)} %get-tuple-element.29, f32[2,2,8,64]{3,2,1,0:T(8,128)S(1)} %get-tuple-element.28), kind=kOutput, calls=%fused_computation.86 | convolution fusion | flops 137890048 | bytes 5513216 | tf_op jit(solution)/shard_map/bkgpj,bjkd->bpkgd/dot_general | solution.py:100
  435.7 1.4 broadcast_multiply_fusion.2
  437.2 0.3 copy-done.15
  437.4 1.5 fusion.65
  438.9 1.8 copy.45
  440.7 0.6 reduce-scatter.3.cloned.1.call-start
  441.3 1.7 slice_negate_fusion.1
  443.0 16.3 %fusion.66 = bf16[2,256,2,128]{3,1,2,0:T(8,128)(2,1)} fusion(bf16[2,64,2,8,128]{4,1,3,2,0:T(8,128)(2,1)} %bitcast.257, f32[2,2,256,64,8]{2,3,4,1,0:T(8,128)} %fusion.96, f32[2,2,8,64,256]{4,3,2,1,0:T(8,128)} %get-tuple-element.29, f32[2,2,8,64]{3,2,1,0:T(8,128)S(1)} %get-tuple-element.28), kind=kOutput, calls=%fused_computation.66 | convolution fusion | flops 138021120 | bytes 4988928 | tf_op jit(solution)/shard_map/bkgpj,bpkgd->bjkd/dot_general | solution.py:103
  459.4 24.7 %all-reduce.11.cloned.1.call-done = bf16[2,256,2,128]{3,2,0,1:T(2,128)(2,1)} async-done(((bf16[2,256,2,128]{3,2,0,1:T(2,128)(2,1)}), bf16[2,256,2,128]{3,2,0,1:T(2,128)(2,1)}) %all-reduce.11.cloned.1.call-update) | async-done | bytes 262160
  484.1 0.9 constant_dynamic-slice_fusion.1
  485.0 5.8 fusion.38
  490.8 20.3 %reduce-scatter.3.cloned.1.call-done = bf16[2,64,2,128]{3,1,2,0:T(8,128)(2,1)} async-done(((bf16[2,256,2,128]{3,1,2,0:T(8,128)(2,1)}), bf16[2,64,2,128]{3,1,2,0:T(8,128)(2,1)}) %reduce-scatter.3.cloned.1.call-update) | async-done | bytes 65552 | tf_op jit(solution)/shard_map/reduce_scatter | solution.py:110
  511.1 0.9 convert_multiply_fusion.6
  512.0 5.8 fusion.42
  517.8 19.2 %fusion.26 = bf16[2,64,8192]{2,1,0:T(8,128)(2,1)} fusion(f32[2,64,8192]{2,1,0:T(8,128)} %fusion.38, f32[2,64,8192]{2,1,0:T(8,128)} %fusion.42, bf16[1,8192,2048]{2,1,0:T(8,128)(2,1)} %param.14, f32[2,64,16,64]{3,1,2,0:T(8,128)} %get-tuple-element.12, f32[2,64,16,64]{3,1,2,0:T(8,128)} %get-tuple-element.11, f32[2,64,16,128]{3,1,2,0:T(8,128)S(1)} %bitcast.242, ...), kind=kOutput, calls=%fused_computation.16 | convolution fusion | flops 4299161600 | bytes 46170112 | tf_op jit(solution)/shard_map/bpc,dc->bpd/dot_general | solution.py:126
  537.1 86.2 %all-reduce.7.cloned.1.call-done = bf16[2,64,8192]{2,1,0:T(8,128)(2,1)} async-done(((bf16[2,64,8192]{2,1,0:T(8,128)(2,1)}), bf16[2,64,8192]{2,1,0:T(8,128)(2,1)}) %all-reduce.7.cloned.1.call-update) | async-done | bytes 2097168 | tf_op jit(solution)/shard_map/psum | solution.py:133
  623.4 2.2 convert_element_type.155
  625.6 2.0 convert_multiply_fusion.1
  627.6 3.4 fusion.144
  631.1 1.3 collective-permute-start
  632.4 2.5 collective-permute-done
  634.9 0.8 copy-done.19
  636.0 44.6 %all-gather.9.cloned.1.call-done = bf16[2,64,8192]{2,1,0:T(8,128)(2,1)} async-done(((bf16[2,64,2048]{2,1,0:T(8,128)(2,1)}), bf16[2,64,8192]{2,1,0:T(8,128)(2,1)}) %all-gather.9.cloned.1.call-update) | async-done | bytes 2097168 | tf_op jit(solution)/shard_map/all_gather | solution.py:48
  680.6 16.4 %fusion.47 = bf16[2,64,2048]{2,1,0:T(8,128)(2,1)S(1)} fusion(bf16[2,64,8192]{2,1,0:T(8,128)(2,1)} %all-gather.9.cloned.1.call-done, bf16[1,2048,8192]{2,1,0:T(8,128)(2,1)} %all-gather.13.cloned.1.call-done), kind=kOutput, calls=%fused_computation.37 | convolution fusion | flops 4295229440 | bytes 36175872 | tf_op jit(solution)/shard_map/bpd,cd->bpc/dot_general | solution.py:69
  697.1 1.8 fusion.93
  698.9 1.5 fusion.63
  700.4 15.6 %fusion.79 = f32[2,2,128,8,64]{2,4,3,1,0:T(8,128)} fusion(f32[2,2,256,64,8]{2,3,4,1,0:T(8,128)} %fusion.93, bf16[2,256,2,128]{3,1,2,0:T(8,128)(2,1)S(1)} %copy-done.21, f32[2,2,8,64,256]{4,3,2,1,0:T(8,128)} %get-tuple-element.29, f32[2,2,8,64]{3,2,1,0:T(8,128)S(1)} %get-tuple-element.28), kind=kOutput, calls=%fused_computation.88 | convolution fusion | flops 137890048 | bytes 5513216 | tf_op jit(solution)/shard_map/bkgpj,bjkd->bpkgd/dot_general | solution.py:100
  716.0 1.3 broadcast_multiply_fusion.1
  717.3 1.8 copy.53
  719.2 1.8 slice_negate_fusion
  721.0 16.3 %fusion.64 = bf16[2,256,2,128]{3,1,2,0:T(8,128)(2,1)} fusion(bf16[2,64,2,8,128]{4,1,3,2,0:T(8,128)(2,1)} %bitcast.258, f32[2,2,256,64,8]{2,3,4,1,0:T(8,128)} %fusion.93, f32[2,2,8,64,256]{4,3,2,1,0:T(8,128)} %get-tuple-element.29, f32[2,2,8,64]{3,2,1,0:T(8,128)S(1)} %get-tuple-element.28), kind=kOutput, calls=%fused_computation.64 | convolution fusion | flops 138021120 | bytes 4988928 | tf_op jit(solution)/shard_map/bkgpj,bpkgd->bjkd/dot_general | solution.py:103
  737.6 23.7 %all-reduce.13.cloned.1.call-done = bf16[2,256,2,128]{3,2,0,1:T(2,128)(2,1)} async-done(((bf16[2,256,2,128]{3,2,0,1:T(2,128)(2,1)}), bf16[2,256,2,128]{3,2,0,1:T(2,128)(2,1)}) %all-reduce.13.cloned.1.call-update) | async-done | bytes 262160
  761.3 0.9 constant_dynamic-slice_fusion
  762.2 5.6 fusion.36
  767.9 20.6 %reduce-scatter.5.cloned.1.call-done = bf16[2,64,2,128]{3,1,2,0:T(8,128)(2,1)} async-done(((bf16[2,256,2,128]{3,1,2,0:T(8,128)(2,1)}), bf16[2,64,2,128]{3,1,2,0:T(8,128)(2,1)}) %reduce-scatter.5.cloned.1.call-update) | async-done | bytes 65552 | tf_op jit(solution)/shard_map/reduce_scatter | solution.py:110
  788.4 0.9 convert_multiply_fusion.4
  789.4 5.8 fusion.40
  795.2 19.3 %fusion.23 = bf16[2,64,8192]{2,1,0:T(8,128)(2,1)} fusion(f32[2,64,8192]{2,1,0:T(8,128)} %fusion.36, f32[2,64,8192]{2,1,0:T(8,128)} %fusion.40, bf16[1,8192,2048]{2,1,0:T(8,128)(2,1)} %param.14, f32[2,64,16,64]{3,1,2,0:T(8,128)} %get-tuple-element.10, f32[2,64,16,64]{3,1,2,0:T(8,128)} %get-tuple-element.9, f32[2,64,16,128]{3,1,2,0:T(8,128)S(1)} %bitcast.240, ...), kind=kOutput, calls=%fused_computation.15 | convolution fusion | flops 4299161600 | bytes 46170112 | tf_op jit(solution)/shard_map/bpc,dc->bpd/dot_general | solution.py:126
  814.6 86.3 %all-reduce.9.cloned.1.call-done = bf16[2,64,8192]{2,1,0:T(8,128)(2,1)} async-done(((bf16[2,64,8192]{2,1,0:T(8,128)(2,1)}), bf16[2,64,8192]{2,1,0:T(8,128)(2,1)}) %all-reduce.9.cloned.1.call-update) | async-done | bytes 2097168 | tf_op jit(solution)/shard_map/psum | solution.py:133
  900.8 2.2 convert_element_type.169
  903.1 0.9 fusion.32
  904.0 0.3 copy-done.10
  904.3 3.1 fusion.70
  (81 shorter events, 2.7 us)
Async XLA Ops:
  6.5 1.0 copy-start
  6.5 58.4 %all-gather.11.cloned.1.call-start = ((), (), s32[]{:S(2)}) async-start(), calls=%async_computation.8 | async-start | bytes 2621440 | tf_op jit(solution)/shard_map/all_gather | solution.py:47
  7.3 108.6 %all-gather.7.cloned.1.call-start = ((), (), s32[]{:S(2)}) async-start(), calls=%async_computation.2 | async-start | bytes 2621440 | tf_op jit(solution)/shard_map/all_gather | solution.py:48
  9.5 391.7 %all-gather.13.cloned.1.call-start = ((), (), s32[]{:S(2)}) async-start(), calls=%async_computation.9 | async-start | bytes 41943040 | tf_op jit(solution)/shard_map/all_gather | solution.py:147
  10.2 473.9 %all-reduce.11.cloned.1.call-start = ((), (), s32[]{:S(2)}) async-start(), calls=%async_computation.10 | async-start | bytes 524288
  56.7 6.4 copy-start.23
  56.7 8.0 copy-start.22
  63.1 4.2 copy-start.17
  64.9 2.4 copy-start.2
  67.4 14.5 %copy-start.9 = (bf16[256,8192]{1,0:T(8,128)(2,1)S(1)}, bf16[256,8192]{1,0:T(8,128)(2,1)}, u32[]{:S(2)}) copy-start(bf16[256,8192]{1,0:T(8,128)(2,1)} %copy.64) | copy-start | bytes 12582916
  81.9 338.3 %copy-start.20 = (bf16[2,256,2,128]{3,1,2,0:T(8,128)(2,1)}, bf16[2,256,2,128]{3,1,2,0:T(8,128)(2,1)S(1)}, u32[]{:S(2)}) copy-start(bf16[2,256,2,128]{3,1,2,0:T(8,128)(2,1)S(1)} %all_gather.23) | copy-start | bytes 786436
  93.1 324.6 %copy-start.11 = (bf16[2,256,2,128]{3,1,2,0:T(8,128)(2,1)}, bf16[2,256,2,128]{3,1,2,0:T(8,128)(2,1)S(1)}, u32[]{:S(2)}) copy-start(bf16[2,256,2,128]{3,1,2,0:T(8,128)(2,1)S(1)} %all_gather.24) | copy-start | bytes 786436
  109.7 2.3 copy-start.18
  417.7 0.8 copy-start.13
  435.7 1.4 copy-start.14
  435.7 1.7 copy-start.15
  440.7 70.3 %reduce-scatter.3.cloned.1.call-start = ((), (), s32[]{:S(2)}) async-start(), calls=%async_computation.3 | async-start | bytes 327680 | tf_op jit(solution)/shard_map/reduce_scatter | solution.py:110
  459.3 164.0 %all-reduce.7.cloned.1.call-start = ((), (), s32[]{:S(2)}) async-start(), calls=%async_computation.4 | async-start | bytes 4194304 | tf_op jit(solution)/shard_map/psum | solution.py:133
  512.0 5.8 copy-start.8
  537.1 143.5 %all-gather.9.cloned.1.call-start = ((), (), s32[]{:S(2)}) async-start(), calls=%async_computation.5 | async-start | bytes 2621440 | tf_op jit(solution)/shard_map/all_gather | solution.py:48
  623.4 2.2 copy-start.6
  627.5 3.4 copy-start.3
  627.5 3.6 copy-start.4
  631.1 3.8 collective-permute-start
  634.9 0.8 copy-start.19
  635.7 61.4 %copy-start.12 = (bf16[2,256,2,128]{3,1,2,0:T(8,128)(2,1)S(1)}, bf16[2,256,2,128]{3,1,2,0:T(8,128)(2,1)}, u32[]{:S(2)}) copy-start(bf16[2,256,2,128]{3,1,2,0:T(8,128)(2,1)} %copy-done.11) | copy-start | bytes 786436
  635.8 125.5 %all-reduce.13.cloned.1.call-start = ((), (), s32[]{:S(2)}) async-start(), calls=%async_computation.11 | async-start | bytes 524288
  697.0 1.9 copy-start.16
  697.1 3.3 copy-start.21
  719.1 69.3 %reduce-scatter.5.cloned.1.call-start = ((), (), s32[]{:S(2)}) async-start(), calls=%async_computation.6 | async-start | bytes 327680 | tf_op jit(solution)/shard_map/reduce_scatter | solution.py:110
  737.3 163.5 %all-reduce.9.cloned.1.call-start = ((), (), s32[]{:S(2)}) async-start(), calls=%async_computation.7 | async-start | bytes 4194304 | tf_op jit(solution)/shard_map/psum | solution.py:133
  789.4 5.8 copy-start.7
  900.8 2.2 copy-start.5
  903.1 1.2 copy-start.10
  904.0 3.4 copy-start.1
Sparse Core Ops, SparseCore 0:
  8.9 48.3 all-gather.10
  58.9 44.4 all-gather.6
  105.3 295.8 all-gather.12
  440.9 43.1 all-reduce.10
  486.7 24.3 reduce-scatter.2
  537.2 86.1 all-reduce.6
  635.9 44.6 all-gather.8
  719.3 41.9 all-reduce.12
  764.1 24.3 reduce-scatter.4
  814.7 86.1 all-reduce.8
where the time goes:
time: 921 us; the launch traced here: 914 us
  waiting for transfers between devices  596 us (65%)
  matrix products  190 us (21%)
  local copies, waits for them, and re-layouts  62 us (7%)
  other arithmetic  29.4 us (3%)
  blocking collectives  20 us (2%)
  between operations  14.8 us (2%)
    all_gather x1, waiting for transfers between devices, on_device(): wo_layer = lax.all_gather(w_out[0], 'dp', axis=1, tiled=True)  285 us
    psum x2, waiting for transfers between devices, layer_grad(): lax.psum(partial_term.astype(jnp.bfloat16), 'tensor').astype(jnp.float32)  172 us
    unnamed x12, waiting for transfers between devices  49.9 us
    all_gather x2, waiting for transfers between devices, layer_grad(): lax.all_gather(own_upstream, 'tensor', axis=2, tiled=True)  44.6 us
    reduce_scatter x2, waiting for transfers between devices, layer_grad(): lax.psum_scatter(key_terms.astype(jnp.bfloat16), 'dp', scatter_dimension=...  40.8 us
    dot_general x1, local copies, waits for them, and re-layouts, layer_grad(): jnp.einsum('bpd,dc->bpc', normed, w_query, preferred_element_type=jnp.flo...  40 us
    dot_general x2, matrix products, layer_grad(): jnp.einsum('bpc,dc->bpd', grad_q, w_query, preferred_element_type=jnp.flo...  38.6 us
    dot_general x2, matrix products, layer_grad(): jnp.einsum('bpd,cd->bpc', g_whole, w_out, preferred_element_type=jnp.floa...  32.7 us
  transfers between devices with their start and end apart: 11, of which 9 were waited for; matrix products, arithmetic and copies ran while one was open for 15% of the time, Pallas kernels for 0%

commit v1 on v0

--- a/solution.py
+++ b/solution.py
@@ -1,3 +1,4 @@
+import functools
 import math
 import jax
 import jax.numpy as jnp
@@ -7,6 +8,24 @@
 HD = 128
 EPS = 1e-05
 THETA = 500000.0
+
+
+def turn_the_kinds(inp, bus_axis):
+    local_now, new = (lax.axis_size(bus_axis), lax.axis_index(bus_axis))
+    v_now, r2 = (inp, 1)
+    while r2 < local_now:
+        made = []
+        for num in tuple(range(local_now)):
+            made.append((num, num ^ r2))
+        moved = lax.ppermute(v_now, bus_axis, made)
+        aux = jnp.concatenate([v_now, moved], axis=1)
+        lower = jnp.concatenate([moved, v_now], axis=1)
+        v_now = jnp.where(new & r2 == 0, aux, lower)
+        r2 = 2 * r2
+    return v_now
+
+
+use_samples = functools.partial(turn_the_kinds, bus_axis="dp")
 
 
 def passed_along(value, axis, steps):
@@ -144,7 +163,7 @@
     wq_layer = w_query[0]
     wk_layer = w_key[0]
     wv_layer = w_value[0]
-    wo_layer = lax.all_gather(w_out[0], "dp", axis=1, tiled=True)
+    wo_layer = use_samples(w_out[0])
     seqs, rows, width_dev = own_input.shape
     section_id = lax.axis_index("section")
     row_ids = lax.axis_index("dp") * rows + jnp.arange(rows, dtype=jnp.int32)

time: 921 us -> 1160 us (1.26)
  blocking collectives: 20 us -> 310 us
  waiting for transfers between devices: 596 us -> 490 us
  matrix products: 190 us -> 224 us
  other arithmetic: 29.4 us -> 47.9 us
    all_gather x1, blocking collectives: 10.4 us -> 301 us  [layer_grad(): lax.all_gather(k_rot, 'dp', axis=1, tiled=True)]
    all_gather x1 -> x0, waiting for transfers between devices: 285 us -> none  [on_device(): wo_layer = lax.all_gather(w_out[0], 'dp', axis=1, tiled=True)]
    ppermute x0 -> x2, waiting for transfers between devices: none -> 181 us  [turn_the_kinds(): moved = lax.ppermute(v_now, bus_axis, made)]
    dot_general x2, matrix products: 32.7 us -> 65 us  [layer_grad(): jnp.einsum('bpd,cd->bpc', g_whole, w_out, preferred_element_type=jnp.floa...]
    select_n x0 -> x1, other arithmetic: none -> 20.5 us  [turn_the_kinds(): v_now = jnp.where(new & r2 == 0, aux, lower)]
    unnamed x12 -> x11, waiting for transfers between devices: 49.9 us -> 48.8 us
  transfers between devices with their start and end apart: 11 -> 12, of which waited for: 9 -> 9; matrix products, arithmetic and copies ran while one was open for 15% -> 12% of each run, Pallas kernels for 0% -> 0%
where the time goes in v1:
time: 1160 us
  waiting for transfers between devices  490 us (42%)
  blocking collectives  310 us (27%)
  matrix products  224 us (19%)
  local copies, waits for them, and re-layouts  63.6 us (5%)
  other arithmetic  47.9 us (4%)
  between operations  14.5 us (1%)
    all_gather x1, blocking collectives, layer_grad(): lax.all_gather(k_rot, 'dp', axis=1, tiled=True)  301 us
    ppermute x2, waiting for transfers between devices, turn_the_kinds(): moved = lax.ppermute(v_now, bus_axis, made)  181 us
    psum x2, waiting for transfers between devices, layer_grad(): lax.psum(partial_term.astype(jnp.bfloat16), 'tensor').astype(jnp.float32)  173 us
    dot_general x2, matrix products, layer_grad(): jnp.einsum('bpd,cd->bpc', g_whole, w_out, preferred_element_type=jnp.floa...  65 us
    unnamed x11, waiting for transfers between devices  48.8 us
    all_gather x2, waiting for transfers between devices, layer_grad(): lax.all_gather(own_upstream, 'tensor', axis=2, tiled=True)  44.6 us
    reduce_scatter x2, waiting for transfers between devices, layer_grad(): lax.psum_scatter(key_terms.astype(jnp.bfloat16), 'dp', scatter_dimension=...  40.9 us
    dot_general x1, local copies, waits for them, and re-layouts, layer_grad(): jnp.einsum('bpd,dc->bpc', normed, w_query, preferred_element_type=jnp.flo...  40.7 us
  transfers between devices with their start and end apart: 12, of which 9 were waited for; matrix products, arithmetic and copies ran while one was open for 12% of the time, Pallas kernels for 0%

profile of v1, /device:TPU:0, one launch (start us, length us, event | category | flops | bytes accessed | tf_op | source)
XLA Modules:
  0.0 1158.0 jit_solution(1821221556518108670)
XLA Ops:
  6.5 3.0 collective-permute-start
  9.5 180.8 %collective-permute-done = bf16[2048,2048]{1,0:T(8,128)(2,1)} collective-permute-done((bf16[2048,2048]{1,0:T(8,128)(2,1)}, bf16[2048,2048]{1,0:T(8,128)(2,1)}, u32[]{:S(2)}, u32[]{:S(2)}) %collective-permute-start) | collective-permute-done | bytes 8388640 | tf_op jit(solution)/shard_map/ppermute | solution.py:20
  190.3 20.5 %maximum_select_fusion.1 = bf16[2048,4096]{1,0:T(8,128)(2,1)} fusion(bf16[2048,2048]{1,0:T(8,128)(2,1)} %collective-permute-done, bf16[2048,2048]{1,0:T(8,128)(2,1)} %bitcast.239, pred[]{:T(512)S(6)} %eq.53), kind=kLoop, calls=%fused_computation.11 | loop fusion | flops 75497472 | bytes 33554432 | tf_op jit(solution)/shard_map/jit(_where)/select_n | solution.py:23
  210.7 1.8 collective-permute-start.1
  212.6 1.3 fusion.51
  214.0 40.7 %copy.63 = bf16[2048,8192]{1,0:T(8,128)(2,1)} copy(bf16[2048,8192]{0,1:T(8,128)(2,1)} %bitcast.234) | data formatting | bytes 67108864 | tf_op jit(solution)/shard_map/bpd,dc->bpc/dot_general | solution.py:76
  254.7 6.4 copy.62
  261.0 6.5 copy.64
  267.5 0.6 dynamic-slice
  269.3 2.1 fusion.34
  271.5 4.5 fusion.118
  276.2 300.6 %all_gather.20 = bf16[2,256,2,128]{3,1,2,0:T(8,128)(2,1)S(1)} all-gather(bf16[2,64,2,128]{3,1,2,0:T(8,128)(2,1)S(1)} %fusion.114), channel_id=1, replica_groups=mesh['dp'=4,'section'=2,'tensor'=4] {'dp'}, dimensions={1}, use_global_device_ids=true | all-gather | bytes 327680 | tf_op jit(solution)/shard_map/all_gather | solution.py:92
  576.9 1.5 convolution_convert_fusion.1
  578.5 9.6 all_gather.21
  588.0 15.8 %fusion.116 = f32[2,64,16,128]{3,1,2,0:T(8,128)S(1)} fusion(bf16[16,128,8192,1]{2,1,0,3:T(8,128)(2,1)} %bitcast.235, bf16[1,2,64,8192]{3,2,1,0:T(8,128)(2,1)S(1)} %copy-done.2, f32[8192]{0:T(1024)S(1)} %bitcast.252, f32[2,64]{1,0:T(2,128)S(1)} %get-tuple-element.23), kind=kOutput, calls=%fused_computation.132 | convolution fusion | flops 4299161600 | bytes 36733440 | tf_op jit(solution)/shard_map/bpd,dc->bpc/dot_general | solution.py:76
  603.8 0.4 slice_negate_fusion.2
  604.2 0.4 fusion.75
  604.6 2.2 fusion.149
  606.9 2.9 fusion.146
  609.8 32.5 %fusion.45 = bf16[2,64,2048]{2,1,0:T(8,128)(2,1)S(1)} fusion(bf16[2,64,8192]{2,1,0:T(8,128)(2,1)} %all-gather.5.cloned.1.call-done, bf16[2048,4096]{1,0:T(8,128)(2,1)} %collective-permute-done.1, bf16[2048,4096]{1,0:T(8,128)(2,1)} %maximum_select_fusion.1, pred[]{:T(512)S(6)} %eq.52), kind=kOutput, calls=%fused_computation.38 | convolution fusion | flops 4446224384 | bytes 36175872 | tf_op jit(solution)/shard_map/bpd,cd->bpc/dot_general | solution.py:88
  642.4 0.8 copy-done.13
  643.2 1.8 fusion.97
  645.0 15.5 %fusion.78 = f32[2,2,128,8,64]{2,4,3,1,0:T(8,128)} fusion(f32[2,2,256,64,8]{2,3,4,1,0:T(8,128)} %fusion.97, bf16[2,256,2,128]{3,1,2,0:T(8,128)(2,1)S(1)} %all_gather.20, f32[2,2,8,64,256]{4,3,2,1,0:T(8,128)} %get-tuple-element.29, f32[2,2,8,64]{3,2,1,0:T(8,128)S(1)} %get-tuple-element.28), kind=kOutput, calls=%fused_computation.87 | convolution fusion | flops 137890048 | bytes 5513216 | tf_op jit(solution)/shard_map/bkgpj,bjkd->bpkgd/dot_general | solution.py:119
  660.5 1.3 broadcast_multiply_fusion.2
  661.8 2.9 fusion.66
  664.7 1.8 copy.45
  666.5 0.6 reduce-scatter.3.cloned.1.call-start
  667.1 1.8 slice_negate_fusion.1
  668.8 16.3 %fusion.67 = bf16[2,256,2,128]{3,1,2,0:T(8,128)(2,1)} fusion(bf16[2,64,2,8,128]{4,1,3,2,0:T(8,128)(2,1)} %bitcast.256, f32[2,2,256,64,8]{2,3,4,1,0:T(8,128)} %fusion.97, f32[2,2,8,64,256]{4,3,2,1,0:T(8,128)} %get-tuple-element.29, f32[2,2,8,64]{3,2,1,0:T(8,128)S(1)} %get-tuple-element.28), kind=kOutput, calls=%fused_computation.67 | convolution fusion | flops 138021120 | bytes 4988928 | tf_op jit(solution)/shard_map/bkgpj,bpkgd->bjkd/dot_general | solution.py:122
  685.2 24.9 %all-reduce.11.cloned.1.call-done = bf16[2,256,2,128]{3,2,0,1:T(2,128)(2,1)} async-done(((bf16[2,256,2,128]{3,2,0,1:T(2,128)(2,1)}), bf16[2,256,2,128]{3,2,0,1:T(2,128)(2,1)}) %all-reduce.11.cloned.1.call-update) | async-done | bytes 262160
  710.0 0.9 constant_dynamic-slice_fusion.1
  711.0 5.6 fusion.39
  716.6 20.4 %reduce-scatter.3.cloned.1.call-done = bf16[2,64,2,128]{3,1,2,0:T(8,128)(2,1)} async-done(((bf16[2,256,2,128]{3,1,2,0:T(8,128)(2,1)}), bf16[2,64,2,128]{3,1,2,0:T(8,128)(2,1)}) %reduce-scatter.3.cloned.1.call-update) | async-done | bytes 65552 | tf_op jit(solution)/shard_map/reduce_scatter | solution.py:129
  737.0 0.9 convert_multiply_fusion.6
  738.0 5.8 fusion.43
  743.8 19.3 %fusion.27 = bf16[2,64,8192]{2,1,0:T(8,128)(2,1)} fusion(f32[2,64,8192]{2,1,0:T(8,128)} %fusion.39, f32[2,64,8192]{2,1,0:T(8,128)} %fusion.43, bf16[1,8192,2048]{2,1,0:T(8,128)(2,1)} %param.14, f32[2,64,16,64]{3,1,2,0:T(8,128)} %get-tuple-element.12, f32[2,64,16,64]{3,1,2,0:T(8,128)} %get-tuple-element.11, f32[2,64,16,128]{3,1,2,0:T(8,128)S(1)} %bitcast.243, ...), kind=kOutput, calls=%fused_computation.17 | convolution fusion | flops 4299161600 | bytes 46170112 | tf_op jit(solution)/shard_map/bpc,dc->bpd/dot_general | solution.py:145
  763.1 86.2 %all-reduce.7.cloned.1.call-done = bf16[2,64,8192]{2,1,0:T(8,128)(2,1)} async-done(((bf16[2,64,8192]{2,1,0:T(8,128)(2,1)}), bf16[2,64,8192]{2,1,0:T(8,128)(2,1)}) %all-reduce.7.cloned.1.call-update) | async-done | bytes 2097168 | tf_op jit(solution)/shard_map/psum | solution.py:152
  849.4 2.2 convert_element_type.155
  851.6 1.9 convert_multiply_fusion.1
  853.5 1.9 copy-done.3
  855.5 2.8 fusion.147
  858.2 1.3 collective-permute-start.2
  859.5 2.5 collective-permute-done.2
  862.0 0.8 copy-done.16
  863.1 44.6 %all-gather.7.cloned.1.call-done = bf16[2,64,8192]{2,1,0:T(8,128)(2,1)} async-done(((bf16[2,64,2048]{2,1,0:T(8,128)(2,1)}), bf16[2,64,8192]{2,1,0:T(8,128)(2,1)}) %all-gather.7.cloned.1.call-update) | async-done | bytes 2097168 | tf_op jit(solution)/shard_map/all_gather | solution.py:67
  907.7 32.5 %fusion.48 = bf16[2,64,2048]{2,1,0:T(8,128)(2,1)S(1)} fusion(bf16[2,64,8192]{2,1,0:T(8,128)(2,1)} %all-gather.7.cloned.1.call-done, bf16[2048,4096]{1,0:T(8,128)(2,1)} %collective-permute-done.1, bf16[2048,4096]{1,0:T(8,128)(2,1)} %maximum_select_fusion.1, pred[]{:T(512)S(6)} %eq.52), kind=kOutput, calls=%fused_computation.39 | convolution fusion | flops 4446224384 | bytes 36175872 | tf_op jit(solution)/shard_map/bpd,cd->bpc/dot_general | solution.py:88
  940.3 1.8 fusion.94
  942.1 2.7 fusion.64
  944.8 15.5 %fusion.80 = f32[2,2,128,8,64]{2,4,3,1,0:T(8,128)} fusion(f32[2,2,256,64,8]{2,3,4,1,0:T(8,128)} %fusion.94, bf16[2,256,2,128]{3,1,2,0:T(8,128)(2,1)S(1)} %copy-done.18, f32[2,2,8,64,256]{4,3,2,1,0:T(8,128)} %get-tuple-element.29, f32[2,2,8,64]{3,2,1,0:T(8,128)S(1)} %get-tuple-element.28), kind=kOutput, calls=%fused_computation.89 | convolution fusion | flops 137890048 | bytes 5513216 | tf_op jit(solution)/shard_map/bkgpj,bjkd->bpkgd/dot_general | solution.py:119
  960.3 1.3 broadcast_multiply_fusion.1
  961.6 1.8 copy.53
  963.5 1.7 slice_negate_fusion
  965.2 16.3 %fusion.65 = bf16[2,256,2,128]{3,1,2,0:T(8,128)(2,1)} fusion(bf16[2,64,2,8,128]{4,1,3,2,0:T(8,128)(2,1)} %bitcast.257, f32[2,2,256,64,8]{2,3,4,1,0:T(8,128)} %fusion.94, f32[2,2,8,64,256]{4,3,2,1,0:T(8,128)} %get-tuple-element.29, f32[2,2,8,64]{3,2,1,0:T(8,128)S(1)} %get-tuple-element.28), kind=kOutput, calls=%fused_computation.65 | convolution fusion | flops 138021120 | bytes 4988928 | tf_op jit(solution)/shard_map/bkgpj,bpkgd->bjkd/dot_general | solution.py:122
  981.9 23.8 %all-reduce.13.cloned.1.call-done = bf16[2,256,2,128]{3,2,0,1:T(2,128)(2,1)} async-done(((bf16[2,256,2,128]{3,2,0,1:T(2,128)(2,1)}), bf16[2,256,2,128]{3,2,0,1:T(2,128)(2,1)}) %all-reduce.13.cloned.1.call-update) | async-done | bytes 262160
  1005.6 0.9 constant_dynamic-slice_fusion
  1006.6 5.6 fusion.37
  1012.2 20.5 %reduce-scatter.5.cloned.1.call-done = bf16[2,64,2,128]{3,1,2,0:T(8,128)(2,1)} async-done(((bf16[2,256,2,128]{3,1,2,0:T(8,128)(2,1)}), bf16[2,64,2,128]{3,1,2,0:T(8,128)(2,1)}) %reduce-scatter.5.cloned.1.call-update) | async-done | bytes 65552 | tf_op jit(solution)/shard_map/reduce_scatter | solution.py:129
  1032.7 0.9 convert_multiply_fusion.4
  1033.7 5.7 fusion.41
  1039.5 19.2 %fusion.24 = bf16[2,64,8192]{2,1,0:T(8,128)(2,1)} fusion(f32[2,64,8192]{2,1,0:T(8,128)} %fusion.37, f32[2,64,8192]{2,1,0:T(8,128)} %fusion.41, bf16[1,8192,2048]{2,1,0:T(8,128)(2,1)} %param.14, f32[2,64,16,64]{3,1,2,0:T(8,128)} %get-tuple-element.10, f32[2,64,16,64]{3,1,2,0:T(8,128)} %get-tuple-element.9, f32[2,64,16,128]{3,1,2,0:T(8,128)S(1)} %bitcast.241, ...), kind=kOutput, calls=%fused_computation.16 | convolution fusion | flops 4299161600 | bytes 46170112 | tf_op jit(solution)/shard_map/bpc,dc->bpd/dot_general | solution.py:145
  1058.7 86.3 %all-reduce.9.cloned.1.call-done = bf16[2,64,8192]{2,1,0:T(8,128)(2,1)} async-done(((bf16[2,64,8192]{2,1,0:T(8,128)(2,1)}), bf16[2,64,8192]{2,1,0:T(8,128)(2,1)}) %all-reduce.9.cloned.1.call-update) | async-done | bytes 2097168 | tf_op jit(solution)/shard_map/psum | solution.py:152
  1145.0 2.2 convert_element_type.169
  1147.2 0.9 fusion.33
  1148.1 3.1 fusion.71
  (79 shorter events, 2.3 us)
Async XLA Ops:
  6.5 206.1 %copy-start = (bf16[2,32,2048]{2,1,0:T(8,128)(2,1)S(1)}, bf16[2,32,2048]{2,1,0:T(8,128)(2,1)}, u32[]{:S(2)}) copy-start(bf16[2,32,2048]{2,1,0:T(8,128)(2,1)} %param.10) | copy-start | bytes 786436
  6.5 262.8 %all-gather.9.cloned.1.call-start = ((), (), s32[]{:S(2)}) async-start(), calls=%async_computation.8 | async-start | bytes 2621440 | tf_op jit(solution)/shard_map/all_gather | solution.py:66
  6.5 183.7 %collective-permute-start = (bf16[2048,2048]{1,0:T(8,128)(2,1)}, bf16[2048,2048]{1,0:T(8,128)(2,1)}, u32[]{:S(2)}, u32[]{:S(2)}) collective-permute-start(bf16[2048,2048]{1,0:T(8,128)(2,1)} %bitcast.238), channel_id=1, source_target_pairs={{0,8},{8,0},{16,24},{24,16},{1,9},{9,1},{17,25},{25,17},{2,10},{10... | collective-permute-start | bytes 25165832 | tf_op jit(solution)/shard_map/ppermute | solution.py:20
  9.5 203.1 %copy-start.19 = (s32[2,32]{1,0:T(2,128)S(1)}, s32[2,32]{1,0:T(2,128)}, u32[]{:S(2)}) copy-start(s32[2,32]{1,0:T(2,128)} %param.11) | copy-start | bytes 772
  210.7 399.0 %collective-permute-start.1 = (bf16[2048,4096]{1,0:T(8,128)(2,1)}, bf16[2048,4096]{1,0:T(8,128)(2,1)}, u32[]{:S(2)}, u32[]{:S(2)}) collective-permute-start(bf16[2048,4096]{1,0:T(8,128)(2,1)} %maximum_select_fusion.1), channel_id=1, source_target_pairs={{0,16},{8,24},{16,0},{24,8},{1,17},{9,25},{17,1},{25,9},{2,18},{10... | collective-permute-start | bytes 50331656 | tf_op jit(solution)/shard_map/ppermute | solution.py:20
  212.5 397.2 %all-gather.5.cloned.1.call-start = ((), (), s32[]{:S(2)}) async-start(), calls=%async_computation.2 | async-start | bytes 2621440 | tf_op jit(solution)/shard_map/all_gather | solution.py:67
  213.9 496.1 %all-reduce.11.cloned.1.call-start = ((), (), s32[]{:S(2)}) async-start(), calls=%async_computation.9 | async-start | bytes 524288
  261.0 6.5 copy-start.21
  261.0 8.0 copy-start.20
  261.0 10.4 copy-start.14
  271.5 305.4 %copy-start.2 = (bf16[1,2,64,8192]{3,2,1,0:T(8,128)(2,1)S(1)}, bf16[1,2,64,8192]{3,2,1,0:T(8,128)(2,1)}, u32[]{:S(2)}) copy-start(bf16[1,2,64,8192]{3,2,1,0:T(8,128)(2,1)} %all-gather.9.cloned.1.call-done) | copy-start | bytes 6291460
  271.5 305.4 %copy-start.9 = (bf16[256,8192]{1,0:T(8,128)(2,1)S(1)}, bf16[256,8192]{1,0:T(8,128)(2,1)}, u32[]{:S(2)}) copy-start(bf16[256,8192]{1,0:T(8,128)(2,1)} %copy.64) | copy-start | bytes 12582916
  576.9 68.1 %copy-start.17 = (bf16[2,256,2,128]{3,1,2,0:T(8,128)(2,1)}, bf16[2,256,2,128]{3,1,2,0:T(8,128)(2,1)S(1)}, u32[]{:S(2)}) copy-start(bf16[2,256,2,128]{3,1,2,0:T(8,128)(2,1)S(1)} %all_gather.20) | copy-start | bytes 786436
  588.0 54.4 %copy-start.11 = (bf16[2,256,2,128]{3,1,2,0:T(8,128)(2,1)}, bf16[2,256,2,128]{3,1,2,0:T(8,128)(2,1)S(1)}, u32[]{:S(2)}) copy-start(bf16[2,256,2,128]{3,1,2,0:T(8,128)(2,1)S(1)} %all_gather.21) | copy-start | bytes 786436
  604.6 37.6 %copy-start.15 = (bf16[2,64,16,128]{3,1,2,0:T(8,128)(2,1)}, bf16[2,64,16,128]{3,1,2,0:T(8,128)(2,1)S(1)}, u32[]{:S(2)}) copy-start(bf16[2,64,16,128]{3,1,2,0:T(8,128)(2,1)S(1)} %fusion.75) | copy-start | bytes 1572868
  642.4 0.8 copy-start.13
  666.5 70.5 %reduce-scatter.3.cloned.1.call-start = ((), (), s32[]{:S(2)}) async-start(), calls=%async_computation.3 | async-start | bytes 327680 | tf_op jit(solution)/shard_map/reduce_scatter | solution.py:129
  685.1 164.2 %all-reduce.7.cloned.1.call-start = ((), (), s32[]{:S(2)}) async-start(), calls=%async_computation.4 | async-start | bytes 4194304 | tf_op jit(solution)/shard_map/psum | solution.py:152
  738.0 5.8 copy-start.8
  763.0 144.6 %all-gather.7.cloned.1.call-start = ((), (), s32[]{:S(2)}) async-start(), calls=%async_computation.5 | async-start | bytes 2621440 | tf_op jit(solution)/shard_map/all_gather | solution.py:67
  849.3 2.2 copy-start.6
  853.5 2.0 copy-start.3
  853.5 4.7 copy-start.4
  858.2 3.8 collective-permute-start.2
  862.0 0.8 copy-start.16
  862.8 77.5 %copy-start.12 = (bf16[2,256,2,128]{3,1,2,0:T(8,128)(2,1)S(1)}, bf16[2,256,2,128]{3,1,2,0:T(8,128)(2,1)}, u32[]{:S(2)}) copy-start(bf16[2,256,2,128]{3,1,2,0:T(8,128)(2,1)} %copy-done.11) | copy-start | bytes 786436
  862.9 142.8 %all-reduce.13.cloned.1.call-start = ((), (), s32[]{:S(2)}) async-start(), calls=%async_computation.10 | async-start | bytes 524288
  940.2 4.6 copy-start.18
  963.5 69.2 %reduce-scatter.5.cloned.1.call-start = ((), (), s32[]{:S(2)}) async-start(), calls=%async_computation.6 | async-start | bytes 327680 | tf_op jit(solution)/shard_map/reduce_scatter | solution.py:129
  981.6 163.4 %all-reduce.9.cloned.1.call-start = ((), (), s32[]{:S(2)}) async-start(), calls=%async_computation.7 | async-start | bytes 4194304 | tf_op jit(solution)/shard_map/psum | solution.py:152
  1033.7 5.7 copy-start.7
  1058.7 89.4 %copy-start.10 = (f32[2,64,2048]{2,1,0:T(8,128)S(1)}, f32[2,64,2048]{2,1,0:T(8,128)}, u32[]{:S(2)}) copy-start(f32[2,64,2048]{2,1,0:T(8,128)} %get-tuple-element.6) | copy-start | bytes 3145732
  1145.0 2.2 copy-start.5
  1145.0 6.2 copy-start.1
Sparse Core Ops, SparseCore 0:
  212.7 45.9 all-gather.8
  260.2 44.4 all-gather.4
  666.6 43.3 all-reduce.10
  712.6 24.3 reduce-scatter.2
  763.2 86.1 all-reduce.6
  863.0 44.6 all-gather.6
  963.6 41.9 all-reduce.12
  1008.4 24.3 reduce-scatter.4
  1058.8 86.1 all-reduce.8
